TPU v7x, 32 devices: a whole 2x2x4 slice. The times are simulated.
32 devices in a mesh: groups: 2 (over y), lon: 4 (over z), lat: 2 (over x), dp: 2 (over core).
Axes of the slice: x: 2, y: 2, z: 4, core: 2. Of those that a mesh axis runs over, the one named last changes fastest.
Arguments:
- fields: bfloat16 [4, 32, 64, 192], P(('groups', 'dp'), 'lat', 'lon'), parts along dimension 0, may hold values from -6 to 6
- cotangent: bfloat16 [4, 32, 64, 192], P(('groups', 'dp'), 'lat', 'lon'), parts along dimension 0, may hold values from -6 to 6
- ocean_mask: int32 [32, 64], P('lat', 'lon'), may hold values from 0 to 1, as said below
- dw_kernel: float32 [7, 7, 192], replicated, may hold values from -0.875 to 0.875
- dw_bias: float32 [192], replicated, may hold values from -4 to 4
- ln_gain: float32 [192], replicated, may hold values from 0.1 to 1.9
- ln_bias: float32 [192], replicated, may hold values from -3 to 3
- w_in: bfloat16 [192, 768], replicated, may hold values from -0.4375 to 0.4375
- b_in: float32 [768], replicated, may hold values from -3 to 3
- w_out: bfloat16 [768, 192], replicated, may hold values from -0.21875 to 0.21875
- b_out: float32 [192], replicated, may hold values from -3 to 3
- layer_scale: float32 [192], replicated, may hold values from 0.3 to 1.5
Outputs:
- block_out: bfloat16 [4, 32, 64, 192], P(('groups', 'dp'), 'lat', 'lon'), parts along dimension 0
- field_grad: bfloat16 [4, 32, 64, 192], P(('groups', 'dp'), 'lat', 'lon'), parts along dimension 0
- grad_kernel: float32 [14, 7, 192], P('groups'), parts along dimension 0
- grad_dw_bias: float32 [384], P('groups'), parts along dimension 0
- grad_ln_gain: float32 [384], P('groups'), parts along dimension 0
- grad_ln_bias: float32 [384], P('groups'), parts along dimension 0
- grad_w_in: float32 [384, 768], P('groups'), parts along dimension 0
- grad_b_in: float32 [1536], P('groups'), parts along dimension 0
- grad_w_out: float32 [1536, 192], P('groups'), parts along dimension 0
- grad_b_out: float32 [384], P('groups'), parts along dimension 0
- grad_scale: float32 [384], P('groups'), parts along dimension 0
There are 2 independent parts, one for each index of `groups`. A program takes and returns all parts, laid end to end along the dimension named above; an argument that names none is the same for every part. Nothing has to cross between parts.
Inputs may be any that keep to these rules, and one draw needn't show every extreme that they name: `ocean_mask`: each device's tile of 16 x 16 cells holds at most 192 ocean cells, and some tile holds exactly 192.
All inputs are finite; a program needn't handle non-finite values.
Results may differ from a plain program's by a relative error of at most 0.0065.
Values may be sent and summed in bfloat16 or wider, within the bound.
No kernel may reach another device: no remote copies, remote signals or barrier semaphores. Data moves between devices by JAX's collectives and lax.ppermute only.
A program may use at most 64 MiB of HBM per device.

v0:
```python
import math
import jax
import jax.numpy as jnp
from jax import lax
from jax.sharding import PartitionSpec as P

EPS = 1e-06


def padded_2(block, sides, width, periodic):
    for axis, dim in sides:
        count = lax.axis_size(axis)
        forward = [(i, i + 1) for i in range(count - 1)]
        if periodic:
            forward.append((count - 1, 0))
        backward = [(target, source) for source, target in forward]
        low = lax.ppermute(
            lax.slice_in_dim(block, block.shape[dim] - width, None, axis=dim), axis, forward
        )
        high = lax.ppermute(lax.slice_in_dim(block, 0, width, axis=dim), axis, backward)
        block = jnp.concatenate([low, block, high], axis=dim)
    return block


def depthwise(padded, kernel, tile_h, tile_w):
    total = jnp.zeros(padded.shape[:-3] + (tile_h, tile_w, padded.shape[-1]), jnp.float32)
    for row_off in range(7):
        for col_off in range(7):
            total = (
                total
                + padded[..., row_off : row_off + tile_h, col_off : col_off + tile_w, :]
                * kernel[row_off, col_off]
            )
    return total


def depthwise_back(padded, kernel, tile_h, tile_w):
    total = jnp.zeros(padded.shape[:-3] + (tile_h, tile_w, padded.shape[-1]), jnp.float32)
    for row_off in range(7):
        for col_off in range(7):
            total = (
                total
                + padded[
                    ..., 6 - row_off : 6 - row_off + tile_h, 6 - col_off : 6 - col_off + tile_w, :
                ]
                * kernel[row_off, col_off]
            )
    return total


def kernel_grad(grad, padded, tile_h, tile_w):
    lead = tuple(range(grad.ndim - 1))
    return jnp.stack(
        [
            jnp.stack(
                [
                    jnp.sum(
                        grad
                        * padded[..., row_off : row_off + tile_h, col_off : col_off + tile_w, :],
                        axis=lead,
                    )
                    for col_off in range(7)
                ]
            )
            for row_off in range(7)
        ]
    )


def gelu_tanh(values):
    return jax.nn.gelu(values, approximate=True)


def mlp_pass(act_rows, out_grad, w_in, b_in, w_out, b_out, layer_scale):
    pre = jnp.dot(act_rows, w_in, preferred_element_type=jnp.float32) + b_in
    hidden, gelu_back = jax.vjp(gelu_tanh, pre)
    hidden_b = hidden.astype(jnp.bfloat16)
    branch = jnp.dot(hidden_b, w_out, preferred_element_type=jnp.float32) + b_out
    branch_grad = out_grad * layer_scale
    branch_b = branch_grad.astype(jnp.bfloat16)
    hidden_grad = jnp.dot(branch_b, w_out.T, preferred_element_type=jnp.float32)
    pre_grad = gelu_back(hidden_grad)[0]
    pre_b = pre_grad.astype(jnp.bfloat16)
    act_grad = jnp.dot(pre_b, w_in.T, preferred_element_type=jnp.float32)
    grads = (
        jnp.dot(act_rows.T, pre_b, preferred_element_type=jnp.float32),
        jnp.sum(pre_grad, axis=0),
        jnp.dot(hidden_b.T, branch_b, preferred_element_type=jnp.float32),
        jnp.sum(branch_grad, axis=0),
        jnp.sum(out_grad * branch, axis=0),
    )
    return (branch, act_grad, grads)


def body(
    fields,
    cotangent,
    ocean_mask,
    dw_kernel,
    dw_bias,
    ln_gain,
    ln_bias,
    w_in,
    b_in,
    w_out,
    b_out,
    layer_scale,
):
    snapshots, tile_h, tile_w, channels = fields.shape
    cells = tile_h * tile_w
    ocean = ocean_mask.astype(jnp.float32)[None, :, :, None]
    start_b = fields * ocean_mask.astype(jnp.bfloat16)[None, :, :, None]
    lat_ext = padded_2(start_b, (("lat", 1),), 3, False)
    padded = padded_2(lat_ext, (("lon", 2),), 3, True).astype(jnp.float32)
    start = start_b.astype(jnp.float32)
    conv_out = depthwise(padded, dw_kernel, tile_h, tile_w) + dw_bias
    center = jnp.mean(conv_out, axis=-1, keepdims=True)
    shifted = conv_out - center
    inv_std = lax.rsqrt(jnp.mean(shifted * shifted, axis=-1, keepdims=True) + EPS)
    normed = shifted * inv_std
    act = (normed * ln_gain + ln_bias).astype(jnp.bfloat16)
    out_grad = cotangent.astype(jnp.float32) * ocean
    flat_branch, flat_act_grad, mlp_sums = mlp_pass(
        act.reshape(-1, channels),
        out_grad.reshape(-1, channels),
        w_in,
        b_in,
        w_out,
        b_out,
        layer_scale,
    )
    branch = flat_branch.reshape(fields.shape)
    act_grad = flat_act_grad.reshape(fields.shape)
    block_out = (ocean * (start + layer_scale * branch)).astype(jnp.bfloat16)
    scaled = act_grad * ln_gain
    conv_grad = inv_std * (
        scaled
        - jnp.mean(scaled, axis=-1, keepdims=True)
        - normed * jnp.mean(scaled * normed, axis=-1, keepdims=True)
    )
    grad_lat = padded_2(conv_grad.astype(jnp.bfloat16), (("lat", 1),), 3, False).astype(
        conv_grad.dtype
    )
    grad_padded = padded_2(grad_lat.astype(jnp.bfloat16), (("lon", 2),), 3, True).astype(
        grad_lat.dtype
    )
    field_grad = (
        ocean * (out_grad + depthwise_back(grad_padded, dw_kernel, tile_h, tile_w))
    ).astype(jnp.bfloat16)
    lead = (0, 1, 2)
    local = (
        kernel_grad(conv_grad, padded, tile_h, tile_w),
        jnp.sum(conv_grad, axis=lead),
        jnp.sum(act_grad * normed, axis=lead),
        jnp.sum(act_grad, axis=lead),
    ) + mlp_sums
    members = lax.axis_size("lon") * lax.axis_size("lat") * lax.axis_size("dp")
    factor = 1.0 / math.sqrt(snapshots * cells * members)
    summed = lax.psum(
        (local[0], local[1], local[2], local[3], local[4], local[5], local[6], local[7], local[8]),
        ("lon", "lat", "dp"),
    )
    finals = [piece * factor for piece in summed]
    return (
        block_out,
        field_grad,
        finals[0],
        finals[1],
        finals[2],
        finals[3],
        finals[4],
        finals[5],
        finals[6],
        finals[7],
        finals[8],
    )


def solution(mesh):
    return jax.shard_map(
        body,
        mesh=mesh,
        in_specs=(
            P(("groups", "dp"), "lat", "lon", None),
            P(("groups", "dp"), "lat", "lon", None),
            P("lat", "lon"),
            P(),
            P(),
            P(),
            P(),
            P(),
            P(),
            P(),
            P(),
            P(),
        ),
        out_specs=(
            P(("groups", "dp"), "lat", "lon", None),
            P(("groups", "dp"), "lat", "lon", None),
            P("groups", None, None),
            P("groups"),
            P("groups"),
            P("groups"),
            P("groups", None),
            P("groups"),
            P("groups", None),
            P("groups"),
            P("groups"),
        ),
        check_vma=False,
    )
```

profile of v0, /device:TPU:0, one launch (start us, length us, event | category | flops | bytes accessed | tf_op | source)
XLA Modules:
  0.0 214.5 jit_solution(16185889891956108017)
XLA Ops:
  7.2 0.0 copy-start
  7.2 0.0 all-reduce.4.cloned.1.call-start
  7.2 0.8 fusion.69
  8.0 1.0 broadcast_multiply_fusion.2
  9.0 0.0 copy-start.6
  9.0 4.9 %collective-permute-start = (bf16[1,3,16,192]{3,2,1,0:T(8,128)(2,1)S(1)}, bf16[1,3,16,192]{3,2,1,0:T(8,128)(2,1)S(1)}, u32[]{:S(2)}, u32[]{:S(2)}) collective-permute-start(bf16[1,3,16,192]{3,2,1,0:T(8,128)(2,1)S(1)} %get-tuple-element.86), channel_id=1, source_target_pairs={{0,2},{1,3},{4,6},{5,7},{8,10},{9,11},{12,14},{13,15},{16,18},{17,... | collective-permute-start | bytes 55304 | tf_op jit(solution)/shard_map/ppermute | solution.py:17
  13.9 1.3 collective-permute-start.1
  15.6 4.1 %collective-permute-done.1 = bf16[1,3,16,192]{3,2,1,0:T(8,128)(2,1)S(1)} collective-permute-done((bf16[1,3,16,192]{3,2,1,0:T(8,128)(2,1)S(1)}, bf16[1,3,16,192]{3,2,1,0:T(8,128)(2,1)S(1)}, u32[]{:S(2)}, u32[]{:S(2)}) %collective-permute-start.1) | collective-permute-done | bytes 18464 | tf_op jit(solution)/shard_map/ppermute | solution.py:20
  19.7 1.6 collective-permute-start.2
  21.3 2.2 %collective-permute-start.3 = (bf16[1,22,3,192]{3,2,1,0:T(4,128)(2,1)S(1)}, bf16[1,22,3,192]{3,2,1,0:T(4,128)(2,1)S(1)}, u32[]{:S(2)}, u32[]{:S(2)}) collective-permute-start(bf16[1,22,3,192]{3,2,1,0:T(4,128)(2,1)S(1)} %get-tuple-element.81), channel_id=1, source_target_pairs={{4,0},{8,4},{12,8},{0,12},{5,1},{9,5},{13,9},{1,13},{6,2},{10,6},{... | collective-permute-start | bytes 76040 | tf_op jit(solution)/shard_map/ppermute | solution.py:20
  23.6 0.6 fusion.68
  24.2 0.0 copy-start.84
  24.2 1.5 collective-permute-done.2
  25.7 0.2 collective-permute-done.3
  25.9 0.1 maximum_convert_fusion
  26.0 0.0 copy-start.90
  26.4 0.3 copy-done.90
  26.7 2.4 %fusion.63 = (f32[16,16]{1,0:T(8,128)S(1)}, f32[1,16,16,192]{3,2,1,0:T(8,128)S(1)}) fusion(f32[192]{0:T(256)S(1)} %copy-done.90, f32[192]{0:T(256)S(1)} %bitcast.228, f32[1,22,22,192]{3,2,1,0:T(8,128)S(1)} %maximum_convert_fusion, f32[192]{0:T(256)} %bitcast.47, f32[192]{0:T(256)S(1)} %bitcast.136, f32[192]{0:T(256)S(1)} %bitcast.138, f32[192]{0:T(256)S(1)} %bitcast.140, ...), kind=kLoop, calls=%fused_computation.208 | loop fusion | flops 4865792 | bytes 9869824 | tf_op jit(solution)/shard_map/reduce_sum | solution.py:117
  29.1 0.2 multiply_reduce_fusion.52
  29.3 0.0 copy-start.86
  29.4 0.1 add_convert_fusion
  29.5 0.6 copy-done.1
  30.1 0.2 convolution_add_fusion
  30.3 0.4 copy-done.94
  30.8 0.4 convolution_add_fusion.1
  31.2 0.0 copy-start.5
  31.2 0.1 copy.27
  31.3 0.7 copy-done.3
  32.1 0.1 copy-done.5
  32.1 1.4 multiply_reduce_fusion
  33.5 1.3 fusion.70
  34.8 1.0 fusion.62
  35.7 0.1 copy.28
  35.9 0.2 multiply_reduce_fusion.1
  36.1 0.1 div.17
  36.2 0.7 multiply_reduce_fusion.2
  36.9 0.6 multiply_reduce_fusion.20
  37.5 0.4 multiply_reduce_fusion.38
  37.9 0.1 copy.29
  38.0 0.6 copy-done.93
  38.6 1.2 fusion.61
  39.8 1.1 fusion.57
  40.9 0.1 multiply_reduce_fusion.53
  41.3 0.5 copy-done.89
  41.8 0.2 copy-done.88
  42.0 0.0 copy-done.87
  42.0 58.4 %all-reduce = (f32[7,7,192]{2,1,0:T(8,128)S(1)}, f32[192]{0:T(256)S(1)}, f32[192]{0:T(256)S(1)}, f32[192]{0:T(256)S(1)}, f32[768]{0:T(1024)S(1)}, /*index=5*/f32[192]{0:T(256)S(1)}, f32[192]{0:T(256)S(1)}) all-reduce(f32[7,7,192]{2,1,0:T(8,128)S(1)} %constant_dynamic-update-s, ...), channel_id=1, replica_groups=mesh['groups'=2,'lon'=4,'lat'=2,'dp'=2] {'lon','lat','dp'}, use_global_device_ids=true, to_apply=%region_53.0 | all-reduce | flops 11136 | bytes 89088 | tf_op jit(solution)/shard_map/psum | solution.py:159
  100.4 0.6 broadcast_multiply_fusion.3
  101.0 0.6 broadcast_multiply_fusion.6
  101.6 1.3 collective-permute-start.4
  102.9 1.3 collective-permute-start.5
  104.2 0.6 broadcast_multiply_fusion.7
  104.8 0.6 broadcast_multiply_fusion.9
  105.3 3.3 %collective-permute-done.5 = bf16[1,3,16,192]{3,2,1,0:T(8,128)(2,1)S(1)} collective-permute-done((bf16[1,3,16,192]{3,2,1,0:T(8,128)(2,1)S(1)}, bf16[1,3,16,192]{3,2,1,0:T(8,128)(2,1)S(1)}, u32[]{:S(2)}, u32[]{:S(2)}) %collective-permute-start.5) | collective-permute-done | bytes 18464 | tf_op jit(solution)/shard_map/ppermute | solution.py:20
  108.7 0.1 collective-permute-start.6
  108.7 3.8 %collective-permute-start.7 = (bf16[1,22,3,192]{3,2,1,0:T(4,128)(2,1)S(1)}, bf16[1,22,3,192]{3,2,1,0:T(4,128)(2,1)S(1)}, u32[]{:S(2)}, u32[]{:S(2)}) collective-permute-start(bf16[1,22,3,192]{3,2,1,0:T(4,128)(2,1)S(1)} %get-tuple-element.79), channel_id=1, source_target_pairs={{4,0},{8,4},{12,8},{0,12},{5,1},{9,5},{13,9},{1,13},{6,2},{10,6},{... | collective-permute-start | bytes 76040 | tf_op jit(solution)/shard_map/ppermute | solution.py:20
  112.5 0.6 broadcast_multiply_fusion.11
  113.1 0.0 all-reduce.4.cloned.1.call-update
  113.5 1.0 collective-permute-done.6
  114.6 0.1 maximum_convert_fusion.1
  115.1 3.3 %fusion.9 = bf16[1,16,16,192]{3,2,1,0:T(8,128)(2,1)} fusion(f32[1,22,22,192]{3,2,1,0:T(8,128)S(1)} %maximum_convert_fusion.1, f32[192]{0:T(256)S(1)} %bitcast.229, f32[192]{0:T(256)} %bitcast.47, f32[192]{0:T(256)S(1)} %bitcast.137, f32[192]{0:T(256)S(1)} %bitcast.139, f32[192]{0:T(256)S(1)} %bitcast.141, f32[192]{0:T(256)S(1)} %bitcast.143, ...), kind=kLoop, calls=%fused_computation.19 | loop fusion | flops 5013504 | bytes 9869056 | tf_op jit(solution)/shard_map/convert_element_type | solution.py:149
  118.4 86.5 %all-reduce.4.cloned.1.call-done = (f32[192,768]{1,0:T(8,128)}, f32[768,192]{0,1:T(8,128)}) async-done(((f32[192,768]{1,0:T(8,128)}, f32[768,192]{0,1:T(8,128)}), (f32[192,768]{1,0:T(8,128)}, f32[768,192]{0,1:T(8,128)})) %all-reduce.4.cloned.1.call-update) | async-done | bytes 1179664 | tf_op jit(solution)/shard_map/psum | solution.py:159
  204.8 2.0 broadcast_multiply_fusion
  206.8 0.9 broadcast_multiply_fusion.1
  (202 shorter events, 0.8 us)
Async XLA Ops:
  7.2 23.2 %copy-start = (bf16[768,192]{0,1:T(8,128)(2,1)S(1)}, bf16[768,192]{0,1:T(8,128)(2,1)}, u32[]{:S(2)}) copy-start(bf16[768,192]{0,1:T(8,128)(2,1)} %param.21) | copy-start | bytes 884740
  7.2 197.7 %all-reduce.4.cloned.1.call-start = ((), (), s32[]{:S(2)}) async-start(), calls=%async_computation | async-start | bytes 2359296 | tf_op jit(solution)/shard_map/psum | solution.py:159
  9.0 6.2 %copy-start.6 = (f32[7,7,192]{2,1,0:T(8,128)S(1)}, f32[7,7,192]{2,1,0:T(8,128)}, u32[]{:S(2)}) copy-start(f32[7,7,192]{2,1,0:T(8,128)} %param.15) | copy-start | bytes 112900
  9.0 6.5 %collective-permute-start = (bf16[1,3,16,192]{3,2,1,0:T(8,128)(2,1)S(1)}, bf16[1,3,16,192]{3,2,1,0:T(8,128)(2,1)S(1)}, u32[]{:S(2)}, u32[]{:S(2)}) collective-permute-start(bf16[1,3,16,192]{3,2,1,0:T(8,128)(2,1)S(1)} %get-tuple-element.86), channel_id=1, source_target_pairs={{0,2},{1,3},{4,6},{5,7},{8,10},{9,11},{12,14},{13,15},{16,18},{17,... | collective-permute-start | bytes 55304 | tf_op jit(solution)/shard_map/ppermute | solution.py:17
  13.9 5.7 %collective-permute-start.1 = (bf16[1,3,16,192]{3,2,1,0:T(8,128)(2,1)S(1)}, bf16[1,3,16,192]{3,2,1,0:T(8,128)(2,1)S(1)}, u32[]{:S(2)}, u32[]{:S(2)}) collective-permute-start(bf16[1,3,16,192]{3,2,1,0:T(8,128)(2,1)S(1)} %get-tuple-element.87), channel_id=1, source_target_pairs={{2,0},{3,1},{6,4},{7,5},{10,8},{11,9},{14,12},{15,13},{18,16},{19,... | collective-permute-start | bytes 55304 | tf_op jit(solution)/shard_map/ppermute | solution.py:20
  15.3 10.7 %copy-start.8 = (f32[1,1,192]{2,1,0:T(1,128)}, f32[1,1,192]{2,1,0:T(1,128)S(1)}, u32[]{:S(2)}) copy-start(f32[1,1,192]{2,1,0:T(1,128)S(1)} %get-tuple-element.97) | copy-start | bytes 2308
  15.3 10.7 %copy-start.10 = (f32[1,1,192]{2,1,0:T(1,128)}, f32[1,1,192]{2,1,0:T(1,128)S(1)}, u32[]{:S(2)}) copy-start(f32[1,1,192]{2,1,0:T(1,128)S(1)} %get-tuple-element.98) | copy-start | bytes 2308
  15.3 10.7 %copy-start.12 = (f32[1,1,192]{2,1,0:T(1,128)}, f32[1,1,192]{2,1,0:T(1,128)S(1)}, u32[]{:S(2)}) copy-start(f32[1,1,192]{2,1,0:T(1,128)S(1)} %get-tuple-element.99) | copy-start | bytes 2308
  15.3 10.7 %copy-start.14 = (f32[1,1,192]{2,1,0:T(1,128)}, f32[1,1,192]{2,1,0:T(1,128)S(1)}, u32[]{:S(2)}) copy-start(f32[1,1,192]{2,1,0:T(1,128)S(1)} %get-tuple-element.100) | copy-start | bytes 2308
  15.3 10.7 %copy-start.16 = (f32[1,1,192]{2,1,0:T(1,128)}, f32[1,1,192]{2,1,0:T(1,128)S(1)}, u32[]{:S(2)}) copy-start(f32[1,1,192]{2,1,0:T(1,128)S(1)} %get-tuple-element.101) | copy-start | bytes 2308
  15.3 10.7 %copy-start.18 = (f32[1,1,192]{2,1,0:T(1,128)}, f32[1,1,192]{2,1,0:T(1,128)S(1)}, u32[]{:S(2)}) copy-start(f32[1,1,192]{2,1,0:T(1,128)S(1)} %get-tuple-element.102) | copy-start | bytes 2308
  15.3 10.7 %copy-start.20 = (f32[1,1,192]{2,1,0:T(1,128)}, f32[1,1,192]{2,1,0:T(1,128)S(1)}, u32[]{:S(2)}) copy-start(f32[1,1,192]{2,1,0:T(1,128)S(1)} %get-tuple-element.103) | copy-start | bytes 2308
  15.3 10.7 %copy-start.22 = (f32[1,1,192]{2,1,0:T(1,128)}, f32[1,1,192]{2,1,0:T(1,128)S(1)}, u32[]{:S(2)}) copy-start(f32[1,1,192]{2,1,0:T(1,128)S(1)} %get-tuple-element.104) | copy-start | bytes 2308
  15.3 10.7 %copy-start.24 = (f32[1,1,192]{2,1,0:T(1,128)}, f32[1,1,192]{2,1,0:T(1,128)S(1)}, u32[]{:S(2)}) copy-start(f32[1,1,192]{2,1,0:T(1,128)S(1)} %get-tuple-element.105) | copy-start | bytes 2308
  15.4 10.7 %copy-start.26 = (f32[1,1,192]{2,1,0:T(1,128)}, f32[1,1,192]{2,1,0:T(1,128)S(1)}, u32[]{:S(2)}) copy-start(f32[1,1,192]{2,1,0:T(1,128)S(1)} %get-tuple-element.106) | copy-start | bytes 2308
  15.4 10.7 %copy-start.28 = (f32[1,1,192]{2,1,0:T(1,128)}, f32[1,1,192]{2,1,0:T(1,128)S(1)}, u32[]{:S(2)}) copy-start(f32[1,1,192]{2,1,0:T(1,128)S(1)} %get-tuple-element.107) | copy-start | bytes 2308
  15.4 10.7 %copy-start.30 = (f32[1,1,192]{2,1,0:T(1,128)}, f32[1,1,192]{2,1,0:T(1,128)S(1)}, u32[]{:S(2)}) copy-start(f32[1,1,192]{2,1,0:T(1,128)S(1)} %get-tuple-element.108) | copy-start | bytes 2308
  15.4 10.7 %copy-start.32 = (f32[1,1,192]{2,1,0:T(1,128)}, f32[1,1,192]{2,1,0:T(1,128)S(1)}, u32[]{:S(2)}) copy-start(f32[1,1,192]{2,1,0:T(1,128)S(1)} %get-tuple-element.109) | copy-start | bytes 2308
  15.4 10.7 %copy-start.34 = (f32[1,1,192]{2,1,0:T(1,128)}, f32[1,1,192]{2,1,0:T(1,128)S(1)}, u32[]{:S(2)}) copy-start(f32[1,1,192]{2,1,0:T(1,128)S(1)} %get-tuple-element.110) | copy-start | bytes 2308
  15.4 10.7 %copy-start.36 = (f32[1,1,192]{2,1,0:T(1,128)}, f32[1,1,192]{2,1,0:T(1,128)S(1)}, u32[]{:S(2)}) copy-start(f32[1,1,192]{2,1,0:T(1,128)S(1)} %get-tuple-element.111) | copy-start | bytes 2308
  15.4 10.7 %copy-start.38 = (f32[1,1,192]{2,1,0:T(1,128)}, f32[1,1,192]{2,1,0:T(1,128)S(1)}, u32[]{:S(2)}) copy-start(f32[1,1,192]{2,1,0:T(1,128)S(1)} %get-tuple-element.112) | copy-start | bytes 2308
  15.5 10.7 %copy-start.40 = (f32[1,1,192]{2,1,0:T(1,128)}, f32[1,1,192]{2,1,0:T(1,128)S(1)}, u32[]{:S(2)}) copy-start(f32[1,1,192]{2,1,0:T(1,128)S(1)} %get-tuple-element.113) | copy-start | bytes 2308
  15.5 10.7 %copy-start.42 = (f32[1,1,192]{2,1,0:T(1,128)}, f32[1,1,192]{2,1,0:T(1,128)S(1)}, u32[]{:S(2)}) copy-start(f32[1,1,192]{2,1,0:T(1,128)S(1)} %get-tuple-element.114) | copy-start | bytes 2308
  15.5 10.7 %copy-start.44 = (f32[1,1,192]{2,1,0:T(1,128)}, f32[1,1,192]{2,1,0:T(1,128)S(1)}, u32[]{:S(2)}) copy-start(f32[1,1,192]{2,1,0:T(1,128)S(1)} %get-tuple-element.115) | copy-start | bytes 2308
  15.5 10.7 %copy-start.46 = (f32[1,1,192]{2,1,0:T(1,128)}, f32[1,1,192]{2,1,0:T(1,128)S(1)}, u32[]{:S(2)}) copy-start(f32[1,1,192]{2,1,0:T(1,128)S(1)} %get-tuple-element.116) | copy-start | bytes 2308
  15.5 10.7 %copy-start.48 = (f32[1,1,192]{2,1,0:T(1,128)}, f32[1,1,192]{2,1,0:T(1,128)S(1)}, u32[]{:S(2)}) copy-start(f32[1,1,192]{2,1,0:T(1,128)S(1)} %get-tuple-element.117) | copy-start | bytes 2308
  15.5 10.7 %copy-start.50 = (f32[1,1,192]{2,1,0:T(1,128)}, f32[1,1,192]{2,1,0:T(1,128)S(1)}, u32[]{:S(2)}) copy-start(f32[1,1,192]{2,1,0:T(1,128)S(1)} %get-tuple-element.118) | copy-start | bytes 2308
  15.5 10.7 %copy-start.52 = (f32[1,1,192]{2,1,0:T(1,128)}, f32[1,1,192]{2,1,0:T(1,128)S(1)}, u32[]{:S(2)}) copy-start(f32[1,1,192]{2,1,0:T(1,128)S(1)} %get-tuple-element.119) | copy-start | bytes 2308
  15.5 10.7 %copy-start.54 = (f32[1,1,192]{2,1,0:T(1,128)}, f32[1,1,192]{2,1,0:T(1,128)S(1)}, u32[]{:S(2)}) copy-start(f32[1,1,192]{2,1,0:T(1,128)S(1)} %get-tuple-element.120) | copy-start | bytes 2308
  15.5 10.7 %copy-start.56 = (f32[1,1,192]{2,1,0:T(1,128)}, f32[1,1,192]{2,1,0:T(1,128)S(1)}, u32[]{:S(2)}) copy-start(f32[1,1,192]{2,1,0:T(1,128)S(1)} %get-tuple-element.121) | copy-start | bytes 2308
  15.5 10.7 %copy-start.58 = (f32[1,1,192]{2,1,0:T(1,128)}, f32[1,1,192]{2,1,0:T(1,128)S(1)}, u32[]{:S(2)}) copy-start(f32[1,1,192]{2,1,0:T(1,128)S(1)} %get-tuple-element.122) | copy-start | bytes 2308
  15.6 10.7 %copy-start.60 = (f32[1,1,192]{2,1,0:T(1,128)}, f32[1,1,192]{2,1,0:T(1,128)S(1)}, u32[]{:S(2)}) copy-start(f32[1,1,192]{2,1,0:T(1,128)S(1)} %get-tuple-element.123) | copy-start | bytes 2308
  15.6 10.7 %copy-start.62 = (f32[1,1,192]{2,1,0:T(1,128)}, f32[1,1,192]{2,1,0:T(1,128)S(1)}, u32[]{:S(2)}) copy-start(f32[1,1,192]{2,1,0:T(1,128)S(1)} %get-tuple-element.124) | copy-start | bytes 2308
  15.6 10.7 %copy-start.64 = (f32[1,1,192]{2,1,0:T(1,128)}, f32[1,1,192]{2,1,0:T(1,128)S(1)}, u32[]{:S(2)}) copy-start(f32[1,1,192]{2,1,0:T(1,128)S(1)} %get-tuple-element.125) | copy-start | bytes 2308
  19.7 6.0 %collective-permute-start.2 = (bf16[1,22,3,192]{3,2,1,0:T(4,128)(2,1)S(1)}, bf16[1,22,3,192]{3,2,1,0:T(4,128)(2,1)S(1)}, u32[]{:S(2)}, u32[]{:S(2)}) collective-permute-start(bf16[1,22,3,192]{3,2,1,0:T(4,128)(2,1)S(1)} %get-tuple-element.80), channel_id=1, source_target_pairs={{0,4},{4,8},{8,12},{12,0},{1,5},{5,9},{9,13},{13,1},{2,6},{6,10},{... | collective-permute-start | bytes 76040 | tf_op jit(solution)/shard_map/ppermute | solution.py:17
  21.3 4.5 %collective-permute-start.3 = (bf16[1,22,3,192]{3,2,1,0:T(4,128)(2,1)S(1)}, bf16[1,22,3,192]{3,2,1,0:T(4,128)(2,1)S(1)}, u32[]{:S(2)}, u32[]{:S(2)}) collective-permute-start(bf16[1,22,3,192]{3,2,1,0:T(4,128)(2,1)S(1)} %get-tuple-element.81), channel_id=1, source_target_pairs={{4,0},{8,4},{12,8},{0,12},{5,1},{9,5},{13,9},{1,13},{6,2},{10,6},{... | collective-permute-start | bytes 76040 | tf_op jit(solution)/shard_map/ppermute | solution.py:20
  24.2 2.1 copy-start.66
  24.2 2.1 copy-start.68
  24.2 2.1 copy-start.70
  24.2 2.1 copy-start.72
  24.2 2.1 %copy-start.74 = (f32[1,1,192]{2,1,0:T(1,128)}, f32[1,1,192]{2,1,0:T(1,128)S(1)}, u32[]{:S(2)}) copy-start(f32[1,1,192]{2,1,0:T(1,128)S(1)} %get-tuple-element.130) | copy-start | bytes 2308
  24.2 2.1 %copy-start.76 = (f32[1,1,192]{2,1,0:T(1,128)}, f32[1,1,192]{2,1,0:T(1,128)S(1)}, u32[]{:S(2)}) copy-start(f32[1,1,192]{2,1,0:T(1,128)S(1)} %get-tuple-element.131) | copy-start | bytes 2308
  24.2 2.1 %copy-start.78 = (f32[1,1,192]{2,1,0:T(1,128)}, f32[1,1,192]{2,1,0:T(1,128)S(1)}, u32[]{:S(2)}) copy-start(f32[1,1,192]{2,1,0:T(1,128)S(1)} %get-tuple-element.132) | copy-start | bytes 2308
  24.2 2.1 %copy-start.80 = (f32[1,1,192]{2,1,0:T(1,128)}, f32[1,1,192]{2,1,0:T(1,128)S(1)}, u32[]{:S(2)}) copy-start(f32[1,1,192]{2,1,0:T(1,128)S(1)} %get-tuple-element.133) | copy-start | bytes 2308
  24.2 2.1 %copy-start.82 = (f32[1,1,192]{2,1,0:T(1,128)}, f32[1,1,192]{2,1,0:T(1,128)S(1)}, u32[]{:S(2)}) copy-start(f32[1,1,192]{2,1,0:T(1,128)S(1)} %get-tuple-element.134) | copy-start | bytes 2308
  24.2 2.1 %copy-start.84 = (f32[1,1,192]{2,1,0:T(1,128)}, f32[1,1,192]{2,1,0:T(1,128)S(1)}, u32[]{:S(2)}) copy-start(f32[1,1,192]{2,1,0:T(1,128)S(1)} %get-tuple-element.135) | copy-start | bytes 2308
  26.7 2.7 %copy-start.7 = (f32[192]{0:T(256)S(1)}, f32[192]{0:T(256)}, u32[]{:S(2)}) copy-start(f32[192]{0:T(256)} %param.17) | copy-start | bytes 2308
  26.7 2.7 %copy-start.91 = (f32[192]{0:T(256)S(1)}, f32[192]{0:T(256)}, u32[]{:S(2)}) copy-start(f32[192]{0:T(256)} %param.18) | copy-start | bytes 2308
  101.6 3.7 %collective-permute-start.4 = (bf16[1,3,16,192]{3,2,1,0:T(8,128)(2,1)S(1)}, bf16[1,3,16,192]{3,2,1,0:T(8,128)(2,1)S(1)}, u32[]{:S(2)}, u32[]{:S(2)}) collective-permute-start(bf16[1,3,16,192]{3,2,1,0:T(8,128)(2,1)S(1)} %get-tuple-element.84), channel_id=1, source_target_pairs={{0,2},{1,3},{4,6},{5,7},{8,10},{9,11},{12,14},{13,15},{16,18},{17,... | collective-permute-start | bytes 55304 | tf_op jit(solution)/shard_map/ppermute | solution.py:17
  102.9 5.7 %collective-permute-start.5 = (bf16[1,3,16,192]{3,2,1,0:T(8,128)(2,1)S(1)}, bf16[1,3,16,192]{3,2,1,0:T(8,128)(2,1)S(1)}, u32[]{:S(2)}, u32[]{:S(2)}) collective-permute-start(bf16[1,3,16,192]{3,2,1,0:T(8,128)(2,1)S(1)} %get-tuple-element.85), channel_id=1, source_target_pairs={{2,0},{3,1},{6,4},{7,5},{10,8},{11,9},{14,12},{15,13},{18,16},{19,... | collective-permute-start | bytes 55304 | tf_op jit(solution)/shard_map/ppermute | solution.py:20
  108.7 5.9 %collective-permute-start.6 = (bf16[1,22,3,192]{3,2,1,0:T(4,128)(2,1)S(1)}, bf16[1,22,3,192]{3,2,1,0:T(4,128)(2,1)S(1)}, u32[]{:S(2)}, u32[]{:S(2)}) collective-permute-start(bf16[1,22,3,192]{3,2,1,0:T(4,128)(2,1)S(1)} %get-tuple-element.78), channel_id=1, source_target_pairs={{0,4},{4,8},{8,12},{12,0},{1,5},{5,9},{9,13},{13,1},{2,6},{6,10},{... | collective-permute-start | bytes 76040 | tf_op jit(solution)/shard_map/ppermute | solution.py:17
  108.7 5.8 %collective-permute-start.7 = (bf16[1,22,3,192]{3,2,1,0:T(4,128)(2,1)S(1)}, bf16[1,22,3,192]{3,2,1,0:T(4,128)(2,1)S(1)}, u32[]{:S(2)}, u32[]{:S(2)}) collective-permute-start(bf16[1,22,3,192]{3,2,1,0:T(4,128)(2,1)S(1)} %get-tuple-element.79), channel_id=1, source_target_pairs={{4,0},{8,4},{12,8},{0,12},{5,1},{9,5},{13,9},{1,13},{6,2},{10,6},{... | collective-permute-start | bytes 76040 | tf_op jit(solution)/shard_map/ppermute | solution.py:20
  113.1 1.6 copy-start.4
  113.1 1.6 copy-start.9
  113.1 1.6 copy-start.11
  113.2 1.6 copy-start.13
  113.2 1.6 copy-start.15
  113.2 1.6 copy-start.17
  113.2 1.6 copy-start.19
  113.2 1.6 copy-start.21
  113.2 1.6 copy-start.23
  113.2 1.6 copy-start.25
  113.2 1.6 copy-start.27
  204.8 2.0 copy-start.2
  (40 other events, 53.5 us)
Sparse Core Ops, SparseCore 0:
  113.2 91.5 all-reduce.3
where the time goes:
time: 215 us
  waiting for transfers between devices  96.5 us (45%)
  blocking collectives  58.4 us (27%)
  other arithmetic  17.3 us (8%)
  starting transfers between devices  16.5 us (8%)
  between operations  15.6 us (7%)
  matrix products  5.21 us (2%)
  local copies, waits for them, and re-layouts  5 us (2%)
    psum x1, waiting for transfers between devices, body(): lax.psum((local[0], local[1], local[2], local[3], local[4], local[5], loc...  86.5 us
    psum x1, blocking collectives, body(): lax.psum((local[0], local[1], local[2], local[3], local[4], local[5], loc...  58.4 us
    ppermute x4, starting transfers between devices, padded_2(): lax.ppermute(lax.slice_in_dim(block, 0, width, axis=dim), axis, backward)  8.64 us
    ppermute x4, starting transfers between devices, padded_2(): lax.ppermute(lax.slice_in_dim(block, block.shape[dim] - width, None, axis...  7.84 us
    ppermute x4, waiting for transfers between devices, padded_2(): lax.ppermute(lax.slice_in_dim(block, 0, width, axis=dim), axis, backward)  7.5 us
    mul x7, other arithmetic, body(): finals = [piece * factor for piece in summed]  5.76 us
  transfers between devices with their start and end apart: 9, of which 6 were waited for; matrix products, arithmetic and copies ran while one was open for 3% of the time, Pallas kernels for 0%

commit v1 on v0

--- a/solution.py
+++ b/solution.py
@@ -157,8 +157,21 @@
     members = lax.axis_size("lon") * lax.axis_size("lat") * lax.axis_size("dp")
     factor = 1.0 / math.sqrt(snapshots * cells * members)
     summed = lax.psum(
-        (local[0], local[1], local[2], local[3], local[4], local[5], local[6], local[7], local[8]),
-        ("lon", "lat", "dp"),
+        lax.psum(
+            (
+                local[0],
+                local[1],
+                local[2],
+                local[3],
+                local[4],
+                local[5],
+                local[6],
+                local[7],
+                local[8],
+            ),
+            "lon",
+        ),
+        ("lat", "dp"),
     )
     finals = [piece * factor for piece in summed]
     return (

time: 215 us -> 156 us (0.73)
  waiting for transfers between devices: 96.5 us -> 60.7 us
  blocking collectives: 58.4 us -> 34.4 us
    psum x1, waiting for transfers between devices: 86.5 us -> 16.8 us  [body(): lax.psum((local[0], local[1], local[2], local[3], local[4], local[5], loc...]
    psum x1, blocking collectives: 58.4 us -> 22 us  [body(): lax.psum((local[0], local[1], local[2], local[3], local[4], local[5], loc...]
    psum x0 -> x1, waiting for transfers between devices: none -> 35.2 us  [body(): lax.psum(lax.psum((local[0], local[1], local[2], local[3], local[4], loca...]
    psum x0 -> x1, blocking collectives: none -> 12.3 us  [body(): lax.psum(lax.psum((local[0], local[1], local[2], local[3], local[4], loca...]
    ppermute x4, waiting for transfers between devices: 7.5 us -> 4.5 us  [padded_2(): lax.ppermute(lax.slice_in_dim(block, 0, width, axis=dim), axis, backward)]
  transfers between devices with their start and end apart: 9 -> 10, of which waited for: 6 -> 7; matrix products, arithmetic and copies ran while one was open for 3% -> 5% of each run, Pallas kernels for 0% -> 0%
where the time goes in v1:
time: 156 us; the launch traced here: 155 us
  waiting for transfers between devices  60.7 us (39%)
  blocking collectives  34.4 us (22%)
  other arithmetic  17.2 us (11%)
  starting transfers between devices  16.9 us (11%)
  between operations  15.6 us (10%)
  local copies, waits for them, and re-layouts  5.45 us (3%)
  matrix products  5.21 us (3%)
    psum x1, waiting for transfers between devices, body(): lax.psum(lax.psum((local[0], local[1], local[2], local[3], local[4], loca...  35.2 us
    psum x1, blocking collectives, body(): lax.psum((local[0], local[1], local[2], local[3], local[4], local[5], loc...  22 us
    psum x1, waiting for transfers between devices, body(): lax.psum((local[0], local[1], local[2], local[3], local[4], local[5], loc...  16.8 us
    psum x1, blocking collectives, body(): lax.psum(lax.psum((local[0], local[1], local[2], local[3], local[4], loca...  12.3 us
    ppermute x4, starting transfers between devices, padded_2(): lax.ppermute(lax.slice_in_dim(block, 0, width, axis=dim), axis, backward)  8.64 us
    ppermute x4, starting transfers between devices, padded_2(): lax.ppermute(lax.slice_in_dim(block, block.shape[dim] - width, None, axis...  8.19 us
    mul x7, other arithmetic, body(): finals = [piece * factor for piece in summed]  5.76 us
    ppermute x4, waiting for transfers between devices, padded_2(): lax.ppermute(lax.slice_in_dim(block, 0, width, axis=dim), axis, backward)  4.5 us
  transfers between devices with their start and end apart: 10, of which 7 were waited for; matrix products, arithmetic and copies ran while one was open for 5% of the time, Pallas kernels for 0%

profile of v1, /device:TPU:0, one launch (start us, length us, event | category | flops | bytes accessed | tf_op | source)
XLA Modules:
  0.0 155.3 jit_solution(12752770792426406468)
XLA Ops:
  7.2 0.0 copy-start
  7.2 0.0 all-reduce.9.cloned.1.call-start
  7.2 0.8 fusion.69
  8.0 1.0 broadcast_multiply_fusion.2
  9.0 4.9 %collective-permute-start = (bf16[1,3,16,192]{3,2,1,0:T(8,128)(2,1)S(1)}, bf16[1,3,16,192]{3,2,1,0:T(8,128)(2,1)S(1)}, u32[]{:S(2)}, u32[]{:S(2)}) collective-permute-start(bf16[1,3,16,192]{3,2,1,0:T(8,128)(2,1)S(1)} %get-tuple-element.95), channel_id=1, source_target_pairs={{0,2},{1,3},{4,6},{5,7},{8,10},{9,11},{12,14},{13,15},{16,18},{17,... | collective-permute-start | bytes 55304 | tf_op jit(solution)/shard_map/ppermute | solution.py:17
  13.9 1.3 collective-permute-start.1
  15.6 4.1 %collective-permute-done.1 = bf16[1,3,16,192]{3,2,1,0:T(8,128)(2,1)S(1)} collective-permute-done((bf16[1,3,16,192]{3,2,1,0:T(8,128)(2,1)S(1)}, bf16[1,3,16,192]{3,2,1,0:T(8,128)(2,1)S(1)}, u32[]{:S(2)}, u32[]{:S(2)}) %collective-permute-start.1) | collective-permute-done | bytes 18464 | tf_op jit(solution)/shard_map/ppermute | solution.py:20
  19.7 1.6 %collective-permute-start.2 = (bf16[1,22,3,192]{3,2,1,0:T(4,128)(2,1)S(1)}, bf16[1,22,3,192]{3,2,1,0:T(4,128)(2,1)S(1)}, u32[]{:S(2)}, u32[]{:S(2)}) collective-permute-start(bf16[1,22,3,192]{3,2,1,0:T(4,128)(2,1)S(1)} %get-tuple-element.89), channel_id=1, source_target_pairs={{0,4},{4,8},{8,12},{12,0},{1,5},{5,9},{9,13},{13,1},{2,6},{6,10},{... | collective-permute-start | bytes 76040 | tf_op jit(solution)/shard_map/ppermute | solution.py:17
  21.3 2.2 %collective-permute-start.3 = (bf16[1,22,3,192]{3,2,1,0:T(4,128)(2,1)S(1)}, bf16[1,22,3,192]{3,2,1,0:T(4,128)(2,1)S(1)}, u32[]{:S(2)}, u32[]{:S(2)}) collective-permute-start(bf16[1,22,3,192]{3,2,1,0:T(4,128)(2,1)S(1)} %get-tuple-element.90), channel_id=1, source_target_pairs={{4,0},{8,4},{12,8},{0,12},{5,1},{9,5},{13,9},{1,13},{6,2},{10,6},{... | collective-permute-start | bytes 76040 | tf_op jit(solution)/shard_map/ppermute | solution.py:20
  23.6 0.5 fusion.68
  24.2 1.5 collective-permute-done.2
  25.7 0.2 collective-permute-done.3
  25.9 0.1 maximum_convert_fusion
  26.4 0.3 copy-done.90
  26.7 2.4 %fusion.63 = (f32[16,16]{1,0:T(8,128)S(1)}, f32[1,16,16,192]{3,2,1,0:T(8,128)S(1)}) fusion(f32[192]{0:T(256)S(1)} %copy-done.90, f32[192]{0:T(256)S(1)} %bitcast.228, f32[1,22,22,192]{3,2,1,0:T(8,128)S(1)} %maximum_convert_fusion, f32[192]{0:T(256)} %bitcast.47, f32[192]{0:T(256)S(1)} %bitcast.136, f32[192]{0:T(256)S(1)} %bitcast.138, f32[192]{0:T(256)S(1)} %bitcast.140, ...), kind=kLoop, calls=%fused_computation.208 | loop fusion | flops 4865792 | bytes 9869824 | tf_op jit(solution)/shard_map/reduce_sum | solution.py:117
  29.0 0.2 multiply_reduce_fusion.52
  29.3 0.1 add_convert_fusion
  29.4 0.6 copy-done.1
  30.0 0.2 convolution_add_fusion
  30.3 0.4 copy-done.94
  30.7 0.4 convolution_add_fusion.1
  31.1 0.1 copy.27
  31.3 0.7 copy-done.3
  32.0 0.1 copy-done.5
  32.1 1.4 multiply_reduce_fusion
  33.5 1.3 fusion.70
  34.7 1.0 fusion.62
  35.7 0.1 copy.28
  35.8 0.2 multiply_reduce_fusion.1
  36.1 0.1 div.17
  36.2 0.7 multiply_reduce_fusion.2
  36.8 0.6 multiply_reduce_fusion.20
  37.4 0.4 multiply_reduce_fusion.38
  37.8 0.1 copy.29
  38.0 0.6 copy-done.93
  38.5 1.2 fusion.61
  39.8 1.1 fusion.57
  40.9 0.1 multiply_reduce_fusion.53
  41.0 1.6 %collective-permute-start.4 = (bf16[1,3,16,192]{3,2,1,0:T(8,128)(2,1)S(1)}, bf16[1,3,16,192]{3,2,1,0:T(8,128)(2,1)S(1)}, u32[]{:S(2)}, u32[]{:S(2)}) collective-permute-start(bf16[1,3,16,192]{3,2,1,0:T(8,128)(2,1)S(1)} %get-tuple-element.93), channel_id=1, source_target_pairs={{0,2},{1,3},{4,6},{5,7},{8,10},{9,11},{12,14},{13,15},{16,18},{17,... | collective-permute-start | bytes 55304 | tf_op jit(solution)/shard_map/ppermute | solution.py:17
  42.6 1.3 collective-permute-start.5
  44.2 0.0 all-reduce.9.cloned.1.call-update
  44.2 0.0 all-reduce.7.cloned.1.call-start
  44.3 0.6 copy-done.89
  44.8 0.1 copy-done.88
  44.9 0.0 copy-done.87
  44.9 22.0 %all-reduce.2 = (f32[7,7,192]{2,1,0:T(8,128)S(1)}, f32[192]{0:T(256)S(1)}, f32[192]{0:T(256)S(1)}, f32[192]{0:T(256)S(1)}, f32[768]{0:T(1024)S(1)}, /*index=5*/f32[192]{0:T(256)S(1)}, f32[192]{0:T(256)S(1)}) all-reduce(f32[7,7,192]{2,1,0:T(8,128)S(1)} %constant_dynamic-update-slice_fusi, ...), channel_id=1, replica_groups=mesh['groups'=2,'lon'=4,'lat'=2,'dp'=2] {'lon'}, use_global_device_ids=true, to_apply=%region_53.0 | all-reduce | flops 11136 | bytes 89088 | tf_op jit(solution)/shard_map/psum | solution.py:160
  67.0 12.3 %all-reduce = (f32[7,7,192]{2,1,0:T(8,128)S(1)}, f32[192]{0:T(256)S(1)}, f32[192]{0:T(256)S(1)}, f32[192]{0:T(256)S(1)}, f32[768]{0:T(1024)S(1)}, /*index=5*/f32[192]{0:T(256)S(1)}, f32[192]{0:T(256)S(1)}) all-reduce(f32[7,7,192]{2,1,0:T(8,128)S(1)} %get-tuple-element.74, ...), channel_id=1, replica_groups=mesh['groups'=2,'lon'=4,'lat'=2,'dp'=2] {'lat','dp'}, use_global_device_ids=true, to_apply=%region_54.0 | all-reduce | flops 11136 | bytes 89088 | tf_op jit(solution)/shard_map/psum | solution.py:159
  79.3 0.6 broadcast_multiply_fusion.7
  79.9 0.6 broadcast_multiply_fusion.6
  80.5 0.6 broadcast_multiply_fusion.3
  81.1 0.6 broadcast_multiply_fusion.9
  81.7 0.1 collective-permute-start.6
  81.8 3.8 %collective-permute-start.7 = (bf16[1,22,3,192]{3,2,1,0:T(4,128)(2,1)S(1)}, bf16[1,22,3,192]{3,2,1,0:T(4,128)(2,1)S(1)}, u32[]{:S(2)}, u32[]{:S(2)}) collective-permute-start(bf16[1,22,3,192]{3,2,1,0:T(4,128)(2,1)S(1)} %get-tuple-element.88), channel_id=1, source_target_pairs={{4,0},{8,4},{12,8},{0,12},{5,1},{9,5},{13,9},{1,13},{6,2},{10,6},{... | collective-permute-start | bytes 76040 | tf_op jit(solution)/shard_map/ppermute | solution.py:20
  85.6 0.6 broadcast_multiply_fusion.11
  86.2 2.7 %collective-permute-done.6 = bf16[1,22,3,192]{3,2,1,0:T(4,128)(2,1)S(1)} collective-permute-done((bf16[1,22,3,192]{3,2,1,0:T(4,128)(2,1)S(1)}, bf16[1,22,3,192]{3,2,1,0:T(4,128)(2,1)S(1)}, u32[]{:S(2)}, u32[]{:S(2)}) %collective-permute-start.6) | collective-permute-done | bytes 25376 | tf_op jit(solution)/shard_map/ppermute | solution.py:17
  88.9 0.3 collective-permute-done.7
  89.1 0.1 maximum_convert_fusion.1
  89.3 16.8 %all-reduce.9.cloned.1.call-done = (f32[192,768]{1,0:T(8,128)}, f32[768,192]{0,1:T(8,128)}) async-done(((f32[192,768]{1,0:T(8,128)}, f32[768,192]{0,1:T(8,128)}), (f32[192,768]{1,0:T(8,128)}, f32[768,192]{0,1:T(8,128)})) %all-reduce.9.cloned.1.call-update) | async-done | bytes 1179664 | tf_op jit(solution)/shard_map/psum | solution.py:160
  106.4 0.0 all-reduce.7.cloned.1.call-update
  106.4 0.5 copy-done.4
  107.3 3.2 %fusion.9 = bf16[1,16,16,192]{3,2,1,0:T(8,128)(2,1)} fusion(f32[1,22,22,192]{3,2,1,0:T(8,128)S(1)} %maximum_convert_fusion.1, f32[192]{0:T(256)S(1)} %bitcast.229, f32[192]{0:T(256)} %bitcast.47, f32[192]{0:T(256)S(1)} %bitcast.137, f32[192]{0:T(256)S(1)} %bitcast.139, f32[192]{0:T(256)S(1)} %bitcast.141, f32[192]{0:T(256)S(1)} %bitcast.143, ...), kind=kLoop, calls=%fused_computation.19 | loop fusion | flops 5013504 | bytes 9869056 | tf_op jit(solution)/shard_map/convert_element_type | solution.py:149
  110.5 35.2 %all-reduce.7.cloned.1.call-done = (f32[192,768]{1,0:T(8,128)}, f32[768,192]{0,1:T(8,128)}) async-done(((f32[192,768]{1,0:T(8,128)}, f32[768,192]{0,1:T(8,128)}), (f32[192,768]{1,0:T(8,128)}, f32[768,192]{0,1:T(8,128)})) %all-reduce.7.cloned.1.call-update) | async-done | bytes 1179664 | tf_op jit(solution)/shard_map/psum | solution.py:159
  145.7 2.0 %broadcast_multiply_fusion = f32[768,192]{0,1:T(8,128)} fusion(f32[768,192]{0,1:T(8,128)} %get-tuple-element.73), kind=kLoop, calls=%fused_computation.11 | loop fusion | flops 147456 | bytes 1179648 | tf_op jit(solution)/shard_map/mul | solution.py:176
  147.6 0.9 broadcast_multiply_fusion.1
  (206 shorter events, 0.8 us)
Async XLA Ops:
  7.2 23.1 %copy-start = (bf16[768,192]{0,1:T(8,128)(2,1)S(1)}, bf16[768,192]{0,1:T(8,128)(2,1)}, u32[]{:S(2)}) copy-start(bf16[768,192]{0,1:T(8,128)(2,1)} %param.21) | copy-start | bytes 884740
  7.2 98.8 %all-reduce.9.cloned.1.call-start = ((), (), s32[]{:S(2)}) async-start(), calls=%async_computation.1 | async-start | bytes 2359296 | tf_op jit(solution)/shard_map/psum | solution.py:160
  9.0 6.2 %copy-start.6 = (f32[7,7,192]{2,1,0:T(8,128)S(1)}, f32[7,7,192]{2,1,0:T(8,128)}, u32[]{:S(2)}) copy-start(f32[7,7,192]{2,1,0:T(8,128)} %param.15) | copy-start | bytes 112900
  9.0 6.5 %collective-permute-start = (bf16[1,3,16,192]{3,2,1,0:T(8,128)(2,1)S(1)}, bf16[1,3,16,192]{3,2,1,0:T(8,128)(2,1)S(1)}, u32[]{:S(2)}, u32[]{:S(2)}) collective-permute-start(bf16[1,3,16,192]{3,2,1,0:T(8,128)(2,1)S(1)} %get-tuple-element.95), channel_id=1, source_target_pairs={{0,2},{1,3},{4,6},{5,7},{8,10},{9,11},{12,14},{13,15},{16,18},{17,... | collective-permute-start | bytes 55304 | tf_op jit(solution)/shard_map/ppermute | solution.py:17
  13.9 5.7 %collective-permute-start.1 = (bf16[1,3,16,192]{3,2,1,0:T(8,128)(2,1)S(1)}, bf16[1,3,16,192]{3,2,1,0:T(8,128)(2,1)S(1)}, u32[]{:S(2)}, u32[]{:S(2)}) collective-permute-start(bf16[1,3,16,192]{3,2,1,0:T(8,128)(2,1)S(1)} %get-tuple-element.96), channel_id=1, source_target_pairs={{2,0},{3,1},{6,4},{7,5},{10,8},{11,9},{14,12},{15,13},{18,16},{19,... | collective-permute-start | bytes 55304 | tf_op jit(solution)/shard_map/ppermute | solution.py:20
  15.3 10.7 %copy-start.8 = (f32[1,1,192]{2,1,0:T(1,128)}, f32[1,1,192]{2,1,0:T(1,128)S(1)}, u32[]{:S(2)}) copy-start(f32[1,1,192]{2,1,0:T(1,128)S(1)} %get-tuple-element.106) | copy-start | bytes 2308
  15.3 10.7 %copy-start.10 = (f32[1,1,192]{2,1,0:T(1,128)}, f32[1,1,192]{2,1,0:T(1,128)S(1)}, u32[]{:S(2)}) copy-start(f32[1,1,192]{2,1,0:T(1,128)S(1)} %get-tuple-element.107) | copy-start | bytes 2308
  15.3 10.7 %copy-start.12 = (f32[1,1,192]{2,1,0:T(1,128)}, f32[1,1,192]{2,1,0:T(1,128)S(1)}, u32[]{:S(2)}) copy-start(f32[1,1,192]{2,1,0:T(1,128)S(1)} %get-tuple-element.108) | copy-start | bytes 2308
  15.3 10.7 %copy-start.14 = (f32[1,1,192]{2,1,0:T(1,128)}, f32[1,1,192]{2,1,0:T(1,128)S(1)}, u32[]{:S(2)}) copy-start(f32[1,1,192]{2,1,0:T(1,128)S(1)} %get-tuple-element.109) | copy-start | bytes 2308
  15.3 10.7 %copy-start.16 = (f32[1,1,192]{2,1,0:T(1,128)}, f32[1,1,192]{2,1,0:T(1,128)S(1)}, u32[]{:S(2)}) copy-start(f32[1,1,192]{2,1,0:T(1,128)S(1)} %get-tuple-element.110) | copy-start | bytes 2308
  15.3 10.7 %copy-start.18 = (f32[1,1,192]{2,1,0:T(1,128)}, f32[1,1,192]{2,1,0:T(1,128)S(1)}, u32[]{:S(2)}) copy-start(f32[1,1,192]{2,1,0:T(1,128)S(1)} %get-tuple-element.111) | copy-start | bytes 2308
  15.3 10.7 %copy-start.20 = (f32[1,1,192]{2,1,0:T(1,128)}, f32[1,1,192]{2,1,0:T(1,128)S(1)}, u32[]{:S(2)}) copy-start(f32[1,1,192]{2,1,0:T(1,128)S(1)} %get-tuple-element.112) | copy-start | bytes 2308
  15.3 10.7 %copy-start.22 = (f32[1,1,192]{2,1,0:T(1,128)}, f32[1,1,192]{2,1,0:T(1,128)S(1)}, u32[]{:S(2)}) copy-start(f32[1,1,192]{2,1,0:T(1,128)S(1)} %get-tuple-element.113) | copy-start | bytes 2308
  15.3 10.7 %copy-start.24 = (f32[1,1,192]{2,1,0:T(1,128)}, f32[1,1,192]{2,1,0:T(1,128)S(1)}, u32[]{:S(2)}) copy-start(f32[1,1,192]{2,1,0:T(1,128)S(1)} %get-tuple-element.114) | copy-start | bytes 2308
  15.4 10.7 %copy-start.26 = (f32[1,1,192]{2,1,0:T(1,128)}, f32[1,1,192]{2,1,0:T(1,128)S(1)}, u32[]{:S(2)}) copy-start(f32[1,1,192]{2,1,0:T(1,128)S(1)} %get-tuple-element.115) | copy-start | bytes 2308
  15.4 10.7 %copy-start.28 = (f32[1,1,192]{2,1,0:T(1,128)}, f32[1,1,192]{2,1,0:T(1,128)S(1)}, u32[]{:S(2)}) copy-start(f32[1,1,192]{2,1,0:T(1,128)S(1)} %get-tuple-element.116) | copy-start | bytes 2308
  15.4 10.7 %copy-start.30 = (f32[1,1,192]{2,1,0:T(1,128)}, f32[1,1,192]{2,1,0:T(1,128)S(1)}, u32[]{:S(2)}) copy-start(f32[1,1,192]{2,1,0:T(1,128)S(1)} %get-tuple-element.117) | copy-start | bytes 2308
  15.4 10.7 %copy-start.32 = (f32[1,1,192]{2,1,0:T(1,128)}, f32[1,1,192]{2,1,0:T(1,128)S(1)}, u32[]{:S(2)}) copy-start(f32[1,1,192]{2,1,0:T(1,128)S(1)} %get-tuple-element.118) | copy-start | bytes 2308
  15.4 10.7 %copy-start.34 = (f32[1,1,192]{2,1,0:T(1,128)}, f32[1,1,192]{2,1,0:T(1,128)S(1)}, u32[]{:S(2)}) copy-start(f32[1,1,192]{2,1,0:T(1,128)S(1)} %get-tuple-element.119) | copy-start | bytes 2308
  15.4 10.7 %copy-start.36 = (f32[1,1,192]{2,1,0:T(1,128)}, f32[1,1,192]{2,1,0:T(1,128)S(1)}, u32[]{:S(2)}) copy-start(f32[1,1,192]{2,1,0:T(1,128)S(1)} %get-tuple-element.120) | copy-start | bytes 2308
  15.4 10.7 %copy-start.38 = (f32[1,1,192]{2,1,0:T(1,128)}, f32[1,1,192]{2,1,0:T(1,128)S(1)}, u32[]{:S(2)}) copy-start(f32[1,1,192]{2,1,0:T(1,128)S(1)} %get-tuple-element.121) | copy-start | bytes 2308
  15.5 10.7 %copy-start.40 = (f32[1,1,192]{2,1,0:T(1,128)}, f32[1,1,192]{2,1,0:T(1,128)S(1)}, u32[]{:S(2)}) copy-start(f32[1,1,192]{2,1,0:T(1,128)S(1)} %get-tuple-element.122) | copy-start | bytes 2308
  15.5 10.7 %copy-start.42 = (f32[1,1,192]{2,1,0:T(1,128)}, f32[1,1,192]{2,1,0:T(1,128)S(1)}, u32[]{:S(2)}) copy-start(f32[1,1,192]{2,1,0:T(1,128)S(1)} %get-tuple-element.123) | copy-start | bytes 2308
  15.5 10.7 %copy-start.44 = (f32[1,1,192]{2,1,0:T(1,128)}, f32[1,1,192]{2,1,0:T(1,128)S(1)}, u32[]{:S(2)}) copy-start(f32[1,1,192]{2,1,0:T(1,128)S(1)} %get-tuple-element.124) | copy-start | bytes 2308
  15.5 10.7 %copy-start.46 = (f32[1,1,192]{2,1,0:T(1,128)}, f32[1,1,192]{2,1,0:T(1,128)S(1)}, u32[]{:S(2)}) copy-start(f32[1,1,192]{2,1,0:T(1,128)S(1)} %get-tuple-element.125) | copy-start | bytes 2308
  15.5 10.7 %copy-start.48 = (f32[1,1,192]{2,1,0:T(1,128)}, f32[1,1,192]{2,1,0:T(1,128)S(1)}, u32[]{:S(2)}) copy-start(f32[1,1,192]{2,1,0:T(1,128)S(1)} %get-tuple-element.126) | copy-start | bytes 2308
  15.5 10.7 %copy-start.50 = (f32[1,1,192]{2,1,0:T(1,128)}, f32[1,1,192]{2,1,0:T(1,128)S(1)}, u32[]{:S(2)}) copy-start(f32[1,1,192]{2,1,0:T(1,128)S(1)} %get-tuple-element.127) | copy-start | bytes 2308
  15.5 10.7 %copy-start.52 = (f32[1,1,192]{2,1,0:T(1,128)}, f32[1,1,192]{2,1,0:T(1,128)S(1)}, u32[]{:S(2)}) copy-start(f32[1,1,192]{2,1,0:T(1,128)S(1)} %get-tuple-element.128) | copy-start | bytes 2308
  15.5 10.7 %copy-start.54 = (f32[1,1,192]{2,1,0:T(1,128)}, f32[1,1,192]{2,1,0:T(1,128)S(1)}, u32[]{:S(2)}) copy-start(f32[1,1,192]{2,1,0:T(1,128)S(1)} %get-tuple-element.129) | copy-start | bytes 2308
  15.5 10.7 %copy-start.56 = (f32[1,1,192]{2,1,0:T(1,128)}, f32[1,1,192]{2,1,0:T(1,128)S(1)}, u32[]{:S(2)}) copy-start(f32[1,1,192]{2,1,0:T(1,128)S(1)} %get-tuple-element.130) | copy-start | bytes 2308
  15.5 10.7 %copy-start.58 = (f32[1,1,192]{2,1,0:T(1,128)}, f32[1,1,192]{2,1,0:T(1,128)S(1)}, u32[]{:S(2)}) copy-start(f32[1,1,192]{2,1,0:T(1,128)S(1)} %get-tuple-element.131) | copy-start | bytes 2308
  15.6 10.7 %copy-start.60 = (f32[1,1,192]{2,1,0:T(1,128)}, f32[1,1,192]{2,1,0:T(1,128)S(1)}, u32[]{:S(2)}) copy-start(f32[1,1,192]{2,1,0:T(1,128)S(1)} %get-tuple-element.132) | copy-start | bytes 2308
  15.6 10.7 %copy-start.62 = (f32[1,1,192]{2,1,0:T(1,128)}, f32[1,1,192]{2,1,0:T(1,128)S(1)}, u32[]{:S(2)}) copy-start(f32[1,1,192]{2,1,0:T(1,128)S(1)} %get-tuple-element.133) | copy-start | bytes 2308
  15.6 10.7 %copy-start.64 = (f32[1,1,192]{2,1,0:T(1,128)}, f32[1,1,192]{2,1,0:T(1,128)S(1)}, u32[]{:S(2)}) copy-start(f32[1,1,192]{2,1,0:T(1,128)S(1)} %get-tuple-element.134) | copy-start | bytes 2308
  19.7 6.0 %collective-permute-start.2 = (bf16[1,22,3,192]{3,2,1,0:T(4,128)(2,1)S(1)}, bf16[1,22,3,192]{3,2,1,0:T(4,128)(2,1)S(1)}, u32[]{:S(2)}, u32[]{:S(2)}) collective-permute-start(bf16[1,22,3,192]{3,2,1,0:T(4,128)(2,1)S(1)} %get-tuple-element.89), channel_id=1, source_target_pairs={{0,4},{4,8},{8,12},{12,0},{1,5},{5,9},{9,13},{13,1},{2,6},{6,10},{... | collective-permute-start | bytes 76040 | tf_op jit(solution)/shard_map/ppermute | solution.py:17
  21.3 4.5 %collective-permute-start.3 = (bf16[1,22,3,192]{3,2,1,0:T(4,128)(2,1)S(1)}, bf16[1,22,3,192]{3,2,1,0:T(4,128)(2,1)S(1)}, u32[]{:S(2)}, u32[]{:S(2)}) collective-permute-start(bf16[1,22,3,192]{3,2,1,0:T(4,128)(2,1)S(1)} %get-tuple-element.90), channel_id=1, source_target_pairs={{4,0},{8,4},{12,8},{0,12},{5,1},{9,5},{13,9},{1,13},{6,2},{10,6},{... | collective-permute-start | bytes 76040 | tf_op jit(solution)/shard_map/ppermute | solution.py:20
  24.1 2.2 %copy-start.66 = (f32[1,1,192]{2,1,0:T(1,128)}, f32[1,1,192]{2,1,0:T(1,128)S(1)}, u32[]{:S(2)}) copy-start(f32[1,1,192]{2,1,0:T(1,128)S(1)} %get-tuple-element.135) | copy-start | bytes 2308
  24.1 2.2 %copy-start.68 = (f32[1,1,192]{2,1,0:T(1,128)}, f32[1,1,192]{2,1,0:T(1,128)S(1)}, u32[]{:S(2)}) copy-start(f32[1,1,192]{2,1,0:T(1,128)S(1)} %get-tuple-element.136) | copy-start | bytes 2308
  24.1 2.2 %copy-start.70 = (f32[1,1,192]{2,1,0:T(1,128)}, f32[1,1,192]{2,1,0:T(1,128)S(1)}, u32[]{:S(2)}) copy-start(f32[1,1,192]{2,1,0:T(1,128)S(1)} %get-tuple-element.137) | copy-start | bytes 2308
  24.1 2.2 %copy-start.72 = (f32[1,1,192]{2,1,0:T(1,128)}, f32[1,1,192]{2,1,0:T(1,128)S(1)}, u32[]{:S(2)}) copy-start(f32[1,1,192]{2,1,0:T(1,128)S(1)} %get-tuple-element.138) | copy-start | bytes 2308
  24.1 2.2 %copy-start.74 = (f32[1,1,192]{2,1,0:T(1,128)}, f32[1,1,192]{2,1,0:T(1,128)S(1)}, u32[]{:S(2)}) copy-start(f32[1,1,192]{2,1,0:T(1,128)S(1)} %get-tuple-element.139) | copy-start | bytes 2308
  24.1 2.2 %copy-start.76 = (f32[1,1,192]{2,1,0:T(1,128)}, f32[1,1,192]{2,1,0:T(1,128)S(1)}, u32[]{:S(2)}) copy-start(f32[1,1,192]{2,1,0:T(1,128)S(1)} %get-tuple-element.140) | copy-start | bytes 2308
  24.1 2.2 %copy-start.78 = (f32[1,1,192]{2,1,0:T(1,128)}, f32[1,1,192]{2,1,0:T(1,128)S(1)}, u32[]{:S(2)}) copy-start(f32[1,1,192]{2,1,0:T(1,128)S(1)} %get-tuple-element.141) | copy-start | bytes 2308
  24.1 2.2 %copy-start.80 = (f32[1,1,192]{2,1,0:T(1,128)}, f32[1,1,192]{2,1,0:T(1,128)S(1)}, u32[]{:S(2)}) copy-start(f32[1,1,192]{2,1,0:T(1,128)S(1)} %get-tuple-element.142) | copy-start | bytes 2308
  24.1 2.2 %copy-start.82 = (f32[1,1,192]{2,1,0:T(1,128)}, f32[1,1,192]{2,1,0:T(1,128)S(1)}, u32[]{:S(2)}) copy-start(f32[1,1,192]{2,1,0:T(1,128)S(1)} %get-tuple-element.143) | copy-start | bytes 2308
  24.2 2.2 %copy-start.84 = (f32[1,1,192]{2,1,0:T(1,128)}, f32[1,1,192]{2,1,0:T(1,128)S(1)}, u32[]{:S(2)}) copy-start(f32[1,1,192]{2,1,0:T(1,128)S(1)} %get-tuple-element.144) | copy-start | bytes 2308
  26.7 2.6 %copy-start.7 = (f32[192]{0:T(256)S(1)}, f32[192]{0:T(256)}, u32[]{:S(2)}) copy-start(f32[192]{0:T(256)} %param.17) | copy-start | bytes 2308
  26.7 2.6 %copy-start.91 = (f32[192]{0:T(256)S(1)}, f32[192]{0:T(256)}, u32[]{:S(2)}) copy-start(f32[192]{0:T(256)} %param.18) | copy-start | bytes 2308
  29.0 1.0 copy-start.1
  31.1 0.9 copy-start.3
  31.1 1.0 copy-start.5
  41.0 40.7 %collective-permute-start.4 = (bf16[1,3,16,192]{3,2,1,0:T(8,128)(2,1)S(1)}, bf16[1,3,16,192]{3,2,1,0:T(8,128)(2,1)S(1)}, u32[]{:S(2)}, u32[]{:S(2)}) collective-permute-start(bf16[1,3,16,192]{3,2,1,0:T(8,128)(2,1)S(1)} %get-tuple-element.93), channel_id=1, source_target_pairs={{0,2},{1,3},{4,6},{5,7},{8,10},{9,11},{12,14},{13,15},{16,18},{17,... | collective-permute-start | bytes 55304 | tf_op jit(solution)/shard_map/ppermute | solution.py:17
  42.6 39.1 %collective-permute-start.5 = (bf16[1,3,16,192]{3,2,1,0:T(8,128)(2,1)S(1)}, bf16[1,3,16,192]{3,2,1,0:T(8,128)(2,1)S(1)}, u32[]{:S(2)}, u32[]{:S(2)}) collective-permute-start(bf16[1,3,16,192]{3,2,1,0:T(8,128)(2,1)S(1)} %get-tuple-element.94), channel_id=1, source_target_pairs={{2,0},{3,1},{6,4},{7,5},{10,8},{11,9},{14,12},{15,13},{18,16},{19,... | collective-permute-start | bytes 55304 | tf_op jit(solution)/shard_map/ppermute | solution.py:20
  44.2 101.5 %all-reduce.7.cloned.1.call-start = ((), (), s32[]{:S(2)}) async-start(), calls=%async_computation | async-start | bytes 2359296 | tf_op jit(solution)/shard_map/psum | solution.py:159
  81.7 7.1 %collective-permute-start.6 = (bf16[1,22,3,192]{3,2,1,0:T(4,128)(2,1)S(1)}, bf16[1,22,3,192]{3,2,1,0:T(4,128)(2,1)S(1)}, u32[]{:S(2)}, u32[]{:S(2)}) collective-permute-start(bf16[1,22,3,192]{3,2,1,0:T(4,128)(2,1)S(1)} %get-tuple-element.87), channel_id=1, source_target_pairs={{0,4},{4,8},{8,12},{12,0},{1,5},{5,9},{9,13},{13,1},{2,6},{6,10},{... | collective-permute-start | bytes 76040 | tf_op jit(solution)/shard_map/ppermute | solution.py:17
  81.8 7.3 %collective-permute-start.7 = (bf16[1,22,3,192]{3,2,1,0:T(4,128)(2,1)S(1)}, bf16[1,22,3,192]{3,2,1,0:T(4,128)(2,1)S(1)}, u32[]{:S(2)}, u32[]{:S(2)}) collective-permute-start(bf16[1,22,3,192]{3,2,1,0:T(4,128)(2,1)S(1)} %get-tuple-element.88), channel_id=1, source_target_pairs={{4,0},{8,4},{12,8},{0,12},{5,1},{9,5},{13,9},{1,13},{6,2},{10,6},{... | collective-permute-start | bytes 76040 | tf_op jit(solution)/shard_map/ppermute | solution.py:20
  106.0 0.9 copy-start.15
  106.0 0.9 copy-start.17
  106.0 0.9 copy-start.19
  106.1 0.9 copy-start.21
  106.1 0.9 copy-start.23
  106.1 0.9 copy-start.25
  106.1 0.9 copy-start.27
  145.7 2.0 %copy-start.2 = (f32[192,768]{1,0:T(8,128)S(1)}, f32[192,768]{1,0:T(8,128)}, u32[]{:S(2)}) copy-start(f32[192,768]{1,0:T(8,128)} %get-tuple-element.72) | copy-start | bytes 1769476
  (41 other events, 35.6 us)
Sparse Core Ops, SparseCore 0:
  44.3 61.6 all-reduce.8
  108.4 37.2 all-reduce.6
